TPU v7x, 256 devices: a whole 4x4x8 slice. The times are simulated.
256 devices in a mesh: dp: 8 (over x, core), ctx: 32 (over z, y).
Axes of the slice: x: 4, y: 4, z: 8, core: 2. Of those that a mesh axis runs over, the one named last changes fastest.
Arguments:
- queries: bfloat16 [8, 8192, 2048], P('dp', 'ctx'), may hold values from -19 to 19
- raw_keys: bfloat16 [8, 8192, 2048], P('dp', 'ctx'), may hold values from -6 to 6
- raw_values: bfloat16 [8, 8192, 2048], P('dp', 'ctx'), may hold values from -6 to 6
- beacon_queries: bfloat16 [8, 64, 2048], P('dp', 'ctx'), may hold values from -19 to 19
- beacon_keys: bfloat16 [8, 64, 2048], P('dp', 'ctx'), may hold values from -6 to 6
- beacon_values: bfloat16 [8, 64, 2048], P('dp', 'ctx'), may hold values from -6 to 6
- upstream: bfloat16 [8, 8192, 2048], P('dp', 'ctx'), may hold values from -6 to 6
- beacon_upstream: bfloat16 [8, 64, 2048], P('dp', 'ctx'), may hold values from -6 to 6
- key_gain: float32 [2048], replicated, may hold values from 0.1 to 1.9
- window: int32 [8], P('dp'), may hold values from 64 to 256, as said below
Outputs:
- grad_queries: bfloat16 [8, 8192, 2048], P('dp', 'ctx')
- grad_keys: bfloat16 [8, 8192, 2048], P('dp', 'ctx')
- grad_values: bfloat16 [8, 8192, 2048], P('dp', 'ctx')
- grad_beacon_queries: bfloat16 [8, 64, 2048], P('dp', 'ctx')
- grad_beacon_keys: bfloat16 [8, 64, 2048], P('dp', 'ctx')
- grad_beacon_values: bfloat16 [8, 64, 2048], P('dp', 'ctx')
- grad_gain: float32 [2048], replicated
Inputs may be any that keep to these rules, and one draw needn't show every extreme that they name: One prompt's window is exactly 256 and one is exactly 64.
All inputs are finite; a program needn't handle non-finite values.
Results may differ from a plain program's by a relative error of at most 0.017.
Values may be sent and summed in bfloat16 or wider, within the bound.
A program may use at most 192 MiB of HBM per device.

v0:
```python
from functools import partial
import math

import jax
import jax.numpy as jnp
from jax import lax
from jax.experimental import pallas as pl
from jax.experimental.pallas import tpu as pltpu
from jax.sharding import PartitionSpec as P

DH = 128
NY = 4
HALF = 128
ROWS = 144
WCOLS = 384
MESH = pl.DeviceIdType.MESH
NEG = -1e30
CONTRACT_LAST = (((1,), (1,)), ((), ()))
CONTRACT_FIRST = (((0,), (0,)), ((), ()))


def dot_t(a, b):
    return lax.dot_general(a, b, CONTRACT_LAST, preferred_element_type=jnp.float32)


def dot_f(a, b):
    return lax.dot_general(a, b, CONTRACT_FIRST, preferred_element_type=jnp.float32)


def dot_n(a, b):
    return jnp.dot(a, b, preferred_element_type=jnp.float32)


def kernel(
    ndp, nctx, heads, window,
    q_hbm, k_hbm, v_hbm, g_hbm, bkv, bqg, gain,
    dq_hbm, dk_hbm, dv_hbm, small, gain_out,
    q_s, k_s, v_s, g_s, dq_s, kv_prev, pg_s, pg_r, own_s, out_s,
    gath, kf, vf, bias_w, bias_b, rs_s, rs_r, zsum, ry_s, ry_r,
    gl, gd_r, gz_s, gz_r, gy_s, gy_r,
    in_sem, out_sem, kv_send, kv_recv, gath_send, gathy_recv, gathz_recv,
    pg_send, pg_recv, rs_send, rs_recv, ry_send, ry_recv,
    gd_send, gd_recv, gz_send, gz_recv, gy_send, gy_recv,
):
    nz = nctx // NY
    nb = 2 * nctx
    groups = heads // 4
    scale = DH ** (-0.5)
    dp = lax.axis_index("dp")
    ctx = lax.axis_index("ctx")
    z = ctx // NY
    y = ctx % NY
    after = (ctx + 1) % nctx
    before = (ctx + nctx - 1) % nctx

    def zpeer(j):
        return ((z + j) % nz) * NY + y

    def ypeer(j):
        return z * NY + (y + j) % NY

    def remote(src, dst, send, recv, to):
        return pltpu.make_async_remote_copy(
            src_ref=src, dst_ref=dst, send_sem=send, recv_sem=recv,
            device_id=to, device_id_type=MESH,
        )

    def drain(ref, sem):
        pltpu.make_async_copy(ref, ref, sem).wait()

    loads = [
        pltpu.make_async_copy(src, dst, in_sem.at[i])
        for i, (src, dst) in enumerate(
            ((q_hbm, q_s), (k_hbm, k_s), (v_hbm, v_s), (g_hbm, g_s))
        )
    ]
    for load in loads:
        load.start()
    own_block = pltpu.make_async_copy(bkv, gath.at[:, ctx], in_sem.at[4])
    own_block.start()

    barrier = pltpu.get_barrier_semaphore()
    pl.semaphore_signal(barrier, inc=1, device_id=(dp, after), device_id_type=MESH)
    pl.semaphore_signal(barrier, inc=1, device_id=(dp, before), device_id_type=MESH)

    @pl.loop(1, NY)
    def _(j):
        pl.semaphore_signal(barrier, inc=1, device_id=(dp, ypeer(j)), device_id_type=MESH)

    @pl.loop(1, nz)
    def _(j):
        pl.semaphore_signal(barrier, inc=1, device_id=(dp, zpeer(j)), device_id_type=MESH)

    @pl.loop(1, ndp)
    def _(j):
        pl.semaphore_signal(
            barrier, inc=1, device_id=((dp + j) % ndp, ctx), device_id_type=MESH
        )

    pl.semaphore_wait(barrier, 2 + NY - 1 + nz - 1 + ndp - 1)

    @pl.loop(1, NY)
    def _(j):
        remote(
            bkv, gath.at[:, ctx], gath_send.at[0], gathy_recv.at[0], (dp, ypeer(j))
        ).start()

    @pl.loop(0, heads)
    def _(h):
        cols = pl.ds(pl.multiple_of(h * DH, DH), DH)
        remote(
            k_hbm.at[:, cols], kv_prev.at[h, 0], kv_send.at[0], kv_recv.at[h], (dp, after)
        ).start()
        remote(
            v_hbm.at[:, cols], kv_prev.at[h, 1], kv_send.at[0], kv_recv.at[h], (dp, after)
        ).start()

    width = window[0]
    for k in range(2):
        row = lax.broadcasted_iota(jnp.int32, (ROWS, WCOLS), 0)
        col = lax.broadcasted_iota(jnp.int32, (ROWS, WCOLS), 1)
        key_position = (ctx - 1) * 2 * HALF + HALF * k + col
        raw = (
            (row < HALF)
            & (col <= 2 * HALF + row)
            & (col > 2 * HALF + row - width)
            & (key_position >= 0)
        )
        beacon = (row == HALF) & (col >= 2 * HALF)
        bias_w[k] = jnp.where(raw | beacon, 0.0, NEG)
        row = lax.broadcasted_iota(jnp.int32, (ROWS, nb), 0)
        col = lax.broadcasted_iota(jnp.int32, (ROWS, nb), 1)
        position = ctx * 2 * HALF + HALF * k + row
        raw = (row < HALF) & (HALF * (col + 1) <= position - width + 1)
        beacon = (row == HALF) & (col <= 2 * ctx + k)
        bias_b[k] = jnp.where(raw | beacon, 0.0, NEG)

    drain(gath.at[:, pl.ds(0, NY - 1)], gathy_recv.at[0])
    own_block.wait()
    for g in range(groups):
        @pl.loop(1, nz)
        def _(j):
            mine = pl.ds(z * NY, NY)
            remote(
                gath.at[g, mine], gath.at[g, mine], gath_send.at[1], gathz_recv.at[g],
                (dp, zpeer(j)),
            ).start()

    for load in loads:
        load.wait()

    first_row = lax.broadcasted_iota(jnp.int32, (16, DH), 0) == 0
    fold = scale * math.log2(math.e)

    @pl.loop(0, groups)
    def _(g):
        drain(gath.at[0, pl.ds(0, (nz - 1) * NY)], gathz_recv.at[g])
        block = gath[g].astype(jnp.float32)
        kf[...] = block[:, 0:8].reshape(nctx * 8, DH)
        vf[...] = block[:, 8:16].reshape(nctx * 8, DH)

        @pl.loop(0, 4)
        def _(hl):
            h = g * 4 + hl
            cols = pl.ds(pl.multiple_of(h * DH, DH), DH)
            raw_b = kf[pl.ds(hl, nb, stride=4), :]
            gained = (raw_b * gain[pl.ds(h, 1), :]).astype(jnp.bfloat16)
            value_b = vf[pl.ds(hl, nb, stride=4), :].astype(jnp.bfloat16)
            drain(kv_prev.at[h], kv_recv.at[h])
            win_k = []
            win_v = []
            for k in range(2):
                win_k.append(
                    jnp.concatenate(
                        [kv_prev[h, 0, HALF * k :], k_s[0 : HALF * (k + 1), cols]], axis=0
                    )
                )
                win_v.append(
                    jnp.concatenate(
                        [kv_prev[h, 1, HALF * k :], v_s[0 : HALF * (k + 1), cols]], axis=0
                    )
                )
            dk_w, dv_w, dk_b, dv_b = [], [], [], []
            for k in range(2):
                extra_q = jnp.where(first_row, bqg[k, pl.ds(h, 1), :], 0.0)
                extra_g = jnp.where(first_row, bqg[2 + k, pl.ds(h, 1), :], 0.0)
                rows = slice(HALF * k, HALF * (k + 1))
                q = jnp.concatenate([q_s[rows, cols], extra_q.astype(jnp.bfloat16)], axis=0)
                up = jnp.concatenate([g_s[rows, cols], extra_g.astype(jnp.bfloat16)], axis=0)
                s_w = dot_t(q, win_k[k]) * fold + bias_w[k]
                s_b = dot_t(q, gained) * fold + bias_b[k]
                peak = jnp.maximum(
                    jnp.max(s_w, axis=1, keepdims=True), jnp.max(s_b, axis=1, keepdims=True)
                )
                e_w = jnp.exp2(s_w - peak)
                e_b = jnp.exp2(s_b - peak)
                total = jnp.sum(e_w, axis=1, keepdims=True) + jnp.sum(
                    e_b, axis=1, keepdims=True
                )
                inverse = 1.0 / total
                p_w = e_w * inverse
                p_b = e_b * inverse
                low_w = p_w.astype(jnp.bfloat16)
                low_b = p_b.astype(jnp.bfloat16)
                dp_w = dot_t(up, win_v[k])
                dp_b = dot_t(up, value_b)
                delta = jnp.sum(
                    low_w.astype(jnp.float32) * dp_w, axis=1, keepdims=True
                ) + jnp.sum(low_b.astype(jnp.float32) * dp_b, axis=1, keepdims=True)
                ds_w = (p_w * (dp_w - delta)).astype(jnp.bfloat16)
                ds_b = (p_b * (dp_b - delta)).astype(jnp.bfloat16)
                dk_w.append(dot_f(ds_w, q))
                dv_w.append(dot_f(low_w, up))
                dk_b.append(dot_f(ds_b, q))
                dv_b.append(dot_f(low_b, up))
                dq = (dot_n(ds_w, win_k[k]) + dot_n(ds_b, gained)) * scale
                dq_s[rows, cols] = dq[0:HALF].astype(jnp.bfloat16)
                gz_s[1 + k, pl.ds(h, 1), :] = dq[HALF : HALF + 1]
            for i, (t, c) in enumerate(((dk_w, scale), (dv_w, 1.0))):
                pg_s[h, i, 0:HALF] = (t[0][0:HALF] * c).astype(jnp.bfloat16)
                pg_s[h, i, HALF:] = (
                    (t[0][HALF : 2 * HALF] + t[1][0:HALF]) * c
                ).astype(jnp.bfloat16)
            part_k = (dk_b[0] + dk_b[1]) * scale
            part_v = dv_b[0] + dv_b[1]
            rs_s[h] = jnp.concatenate(
                [part_k.reshape(nz, 8, DH), part_v.reshape(nz, 8, DH)], axis=1
            ).astype(jnp.bfloat16)
            gl[pl.ds(h, 1), :] = jnp.sum(raw_b * part_k, axis=0, keepdims=True)
            for i, (t, c) in enumerate(((dk_w, scale), (dv_w, 1.0))):
                own_s[h, i, 0:HALF] = (t[0][2 * HALF :] + t[1][HALF : 2 * HALF]) * c
                own_s[h, i, HALF:] = t[1][2 * HALF :] * c
            remote(
                pg_s.at[h], pg_r.at[h], pg_send.at[0], pg_recv.at[h], (dp, before)
            ).start()

            @pl.loop(1, nz)
            def _(j):
                remote(
                    rs_s.at[h, (z + j) % nz], rs_r.at[h, z], rs_send.at[0], rs_recv.at[0],
                    (dp, zpeer(j)),
                ).start()

    store_q = pltpu.make_async_copy(dq_s, dq_hbm, out_sem.at[0])
    store_q.start()

    @pl.loop(1, ndp)
    def _(j):
        remote(
            gl, gd_r.at[dp], gd_send.at[0], gd_recv.at[0], ((dp + j) % ndp, ctx)
        ).start()

    gd_r[dp] = gl[...]
    rs_r[:, z] = rs_s[:, z]

    drain(rs_r.at[:, pl.ds(0, nz - 1)], rs_recv.at[0])
    zsum[...] = jnp.sum(rs_r[...].astype(jnp.float32), axis=1).reshape(heads * 16, DH)
    for t in range(NY):
        for kv in range(2):
            for k in range(2):
                ry_s[t, 2 * kv + k] = zsum[
                    pl.ds(kv * 8 + 2 * t + k, heads, stride=16), :
                ].astype(jnp.bfloat16)

    @pl.loop(1, NY)
    def _(j):
        remote(
            ry_s.at[(y + j) % NY], ry_r.at[y], ry_send.at[0], ry_recv.at[0], (dp, ypeer(j))
        ).start()

    ry_r[y] = ry_s[y]

    drain(gd_r.at[pl.ds(0, ndp - 1)], gd_recv.at[0])
    gz_s[0] = jnp.sum(gd_r[...], axis=0)
    gz_r[z] = gz_s[0]

    @pl.loop(1, nz)
    def _(j):
        remote(
            gz_s.at[0], gz_r.at[z], gz_send.at[0], gz_recv.at[0], (dp, zpeer(j))
        ).start()

    @pl.loop(0, heads)
    def _(h):
        cols = pl.ds(pl.multiple_of(h * DH, DH), DH)
        drain(pg_r.at[h], pg_recv.at[h])
        total = own_s[h] + pg_r[h].astype(jnp.float32)
        out_s[0, :, cols] = total[0].astype(jnp.bfloat16)
        out_s[1, :, cols] = total[1].astype(jnp.bfloat16)
        pltpu.make_async_copy(
            out_s.at[0, :, cols], dk_hbm.at[:, cols], out_sem.at[1]
        ).start()
        pltpu.make_async_copy(
            out_s.at[1, :, cols], dv_hbm.at[:, cols], out_sem.at[2]
        ).start()

    drain(gz_r.at[pl.ds(0, nz - 1)], gz_recv.at[0])
    gy_s[...] = jnp.sum(gz_r[...], axis=0)
    gy_r[y] = gy_s[...]

    @pl.loop(1, NY)
    def _(j):
        remote(gy_s, gy_r.at[y], gy_send.at[0], gy_recv.at[0], (dp, ypeer(j))).start()

    drain(ry_r.at[pl.ds(0, NY - 1)], ry_recv.at[0])
    own = jnp.sum(ry_r[...].astype(jnp.float32), axis=0)
    for k in range(2):
        small[k] = gz_s[1 + k].astype(jnp.bfloat16)
        small[2 + k] = (own[k] * gain[...]).astype(jnp.bfloat16)
        small[4 + k] = own[2 + k].astype(jnp.bfloat16)
    drain(gy_r.at[pl.ds(0, NY - 1)], gy_recv.at[0])
    gain_out[...] = jnp.sum(gy_r[...], axis=0)

    drain(gath.at[:, pl.ds(0, NY - 1)], gath_send.at[0])
    drain(gath.at[:, pl.ds(0, (nz - 1) * NY)], gath_send.at[1])
    drain(kv_prev, kv_send.at[0])
    drain(pg_s, pg_send.at[0])
    drain(rs_s.at[:, pl.ds(0, nz - 1)], rs_send.at[0])
    drain(ry_s.at[pl.ds(0, NY - 1)], ry_send.at[0])
    drain(gd_r.at[pl.ds(0, ndp - 1)], gd_send.at[0])
    drain(gz_r.at[pl.ds(0, nz - 1)], gz_send.at[0])
    drain(gy_r.at[pl.ds(0, NY - 1)], gy_send.at[0])
    store_q.wait()
    drain(dk_hbm, out_sem.at[1])
    drain(dv_hbm, out_sem.at[2])


def on_device(
    queries, raw_keys, raw_values, beacon_queries, beacon_keys, beacon_values,
    upstream, beacon_upstream, key_gain, window,
):
    ndp = lax.axis_size("dp")
    nctx = lax.axis_size("ctx")
    nz = nctx // NY
    nb = 2 * nctx
    slab = queries.shape[1]
    hd = queries.shape[2]
    heads = hd // DH
    groups = heads // 4
    bf16, f32 = jnp.bfloat16, jnp.float32

    def grouped(block):
        return block.reshape(2, groups, 4, DH).transpose(1, 0, 2, 3).reshape(groups, 8, DH)

    bkv = jnp.concatenate([grouped(beacon_keys), grouped(beacon_values)], axis=1)
    bqg = jnp.concatenate([beacon_queries[0], beacon_upstream[0]], axis=0)
    bqg = bqg.astype(f32).reshape(4, heads, DH)
    vmem = pl.BlockSpec(memory_space=pltpu.VMEM)
    anyspace = pl.BlockSpec(memory_space=pl.ANY)
    dma = pltpu.SemaphoreType.DMA
    big = jax.ShapeDtypeStruct((slab, hd), bf16)
    outs = pl.pallas_call(
        partial(kernel, ndp, nctx, heads),
        out_shape=(
            big, big, big,
            jax.ShapeDtypeStruct((6, heads, DH), bf16),
            jax.ShapeDtypeStruct((heads, DH), f32),
        ),
        in_specs=[pl.BlockSpec(memory_space=pltpu.SMEM)] + [anyspace] * 4 + [vmem] * 3,
        out_specs=(anyspace, anyspace, anyspace, vmem, vmem),
        scratch_shapes=[
            pltpu.VMEM((slab, hd), bf16),
            pltpu.VMEM((slab, hd), bf16),
            pltpu.VMEM((slab, hd), bf16),
            pltpu.VMEM((slab, hd), bf16),
            pltpu.VMEM((slab, hd), bf16),
            pltpu.VMEM((heads, 2, slab, DH), bf16),
            pltpu.VMEM((heads, 2, slab, DH), bf16),
            pltpu.VMEM((heads, 2, slab, DH), bf16),
            pltpu.VMEM((heads, 2, slab, DH), f32),
            pltpu.VMEM((2, slab, hd), bf16),
            pltpu.VMEM((groups, nctx, 16, DH), bf16),
            pltpu.VMEM((nctx * 8, DH), f32),
            pltpu.VMEM((nctx * 8, DH), f32),
            pltpu.VMEM((2, ROWS, WCOLS), f32),
            pltpu.VMEM((2, ROWS, nb), f32),
            pltpu.VMEM((heads, nz, 16, DH), bf16),
            pltpu.VMEM((heads, nz, 16, DH), bf16),
            pltpu.VMEM((heads * 16, DH), f32),
            pltpu.VMEM((NY, 4, heads, DH), bf16),
            pltpu.VMEM((NY, 4, heads, DH), bf16),
            pltpu.VMEM((heads, DH), f32),
            pltpu.VMEM((ndp, heads, DH), f32),
            pltpu.VMEM((3, heads, DH), f32),
            pltpu.VMEM((nz, heads, DH), f32),
            pltpu.VMEM((heads, DH), f32),
            pltpu.VMEM((NY, heads, DH), f32),
            dma((5,)), dma((3,)), dma((1,)), dma((heads,)), dma((2,)), dma((1,)),
            dma((groups,)), dma((1,)), dma((heads,)), dma((1,)), dma((1,)), dma((1,)),
            dma((1,)), dma((1,)), dma((1,)), dma((1,)), dma((1,)), dma((1,)), dma((1,)),
        ],
        compiler_params=pltpu.CompilerParams(
            collective_id=0, has_side_effects=True, vmem_limit_bytes=56 * 1024 * 1024
        ),
        name="beacon_backward",
    )(
        window, queries[0], raw_keys[0], raw_values[0], upstream[0], bkv, bqg,
        key_gain.reshape(heads, DH),
    )
    dq, dk, dv, small, gain = outs
    small = small.reshape(3, 1, 2, hd)
    return dq[None], dk[None], dv[None], small[0], small[1], small[2], gain.reshape(hd)


def solution(mesh):
    slabs = P("dp", "ctx", None)
    return jax.shard_map(
        on_device,
        mesh=mesh,
        in_specs=(slabs,) * 8 + (P(), P("dp")),
        out_specs=(slabs,) * 6 + (P(),),
        check_vma=False,
    )
```

profile of v0, /device:TPU:2, one launch (start us, length us, event | category | flops | bytes accessed | tf_op | source)
XLA Modules:
  0.0 125.1 jit_solution(16971465281414416974)
XLA Ops:
  0.6 0.0 copy-start.2
  1.3 0.0 copy-done.2
  1.3 0.0 copy-start.3
  1.4 0.7 copy-done.3
  2.1 0.0 copy-start.5
  2.1 0.0 copy-start.6
  2.1 0.6 pad_maximum_fusion.bkv
  2.7 0.1 copy-done.5
  2.8 0.0 copy-done.6
  2.8 0.6 maximum_convert_fusion.bqg
  3.4 113.5 %beacon_backward.1 = (bf16[256,2048]{1,0:T(8,128)(2,1)}, bf16[256,2048]{1,0:T(8,128)(2,1)}, bf16[256,2048]{1,0:T(8,128)(2,1)}, bf16[6,16,128]{2,1,0:T(8,128)(2,1)}, f32[16,128]{1,0:T(8,128)}) custom-call(s32[1]{0:T(128)S(6)} %copy.27.window, bf16[256,2048]{1,0:T(8,128)(2,1)} %bitcast.23, bf16[256,2048]{1,0:T(8,128)(2,1)} %bitcast.24, ...), custom_call_target="tpu_custom_call" | custom-call | tf_op jit(solution)/shard_map/beacon_backward/pallas_call | solution.py:352
  116.9 0.7 fusion
  117.6 0.6 squeeze.29
  118.3 0.6 squeeze.28
  118.9 0.6 squeeze.27
  119.5 0.0 copy-start.1
  119.5 2.4 %copy.28 = bf16[1,256,2048]{2,1,0:T(8,128)(2,1)} copy(bf16[1,256,2048]{2,1,0:T(8,128)(2,1)} %bitcast.29) | data formatting | bytes 2097152
  121.9 0.0 copy-done.1
  121.9 0.0 copy-start
  121.9 1.0 copy.29
  122.8 0.6 copy-done
  123.5 0.0 copy-start.4
  123.5 1.0 copy.30
  124.4 0.0 copy-done.4
  124.5 0.6 copy.31
  (5 shorter events, 0.0 us)
Async XLA Ops:
  0.6 0.7 copy-start.2
  1.3 0.7 copy-start.3
  2.1 0.7 copy-start.5
  2.1 0.7 copy-start.6
  119.5 2.4 %copy-start.1 = (bf16[256,2048]{1,0:T(8,128)(2,1)S(1)}, bf16[256,2048]{1,0:T(8,128)(2,1)}, u32[]{:S(2)}) copy-start(bf16[256,2048]{1,0:T(8,128)(2,1)} %get-tuple-element.13) | copy-start | bytes 3145732
  121.9 1.6 %copy-start = (bf16[256,2048]{1,0:T(8,128)(2,1)S(1)}, bf16[256,2048]{1,0:T(8,128)(2,1)}, u32[]{:S(2)}) copy-start(bf16[256,2048]{1,0:T(8,128)(2,1)} %get-tuple-element.14) | copy-start | bytes 3145732
  123.5 1.0 copy-start.4
where the time goes:
time: 126 us; the launch traced here: 125 us
  Pallas kernels  113 us (90%)
  local copies, waits for them, and re-layouts  8.97 us (7%)
  between operations  1.35 us (1%)
    pallas_call x1, Pallas kernels, on_device(): pl.pallas_call(partial(kernel, ndp, nctx, heads), out_shape=(big, big, bi...  113 us
    unnamed x18, local copies, waits for them, and re-layouts  6.37 us

commit v1 on v0

--- a/solution.py
+++ b/solution.py
@@ -12,6 +12,8 @@
 NY = 4
 HALF = 128
 ROWS = 144
+AHEAD = 2
+LAST = 3
 WCOLS = 384
 MESH = pl.DeviceIdType.MESH
 NEG = -1e30
@@ -34,11 +36,11 @@
 def kernel(
     ndp, nctx, heads, window,
     q_hbm, k_hbm, v_hbm, g_hbm, bkv, bqg, gain,
-    dq_hbm, dk_hbm, dv_hbm, small, gain_out,
-    q_s, k_s, v_s, g_s, dq_s, kv_prev, pg_s, pg_r, own_s, out_s,
+    dq_out, dk_out, dv_out, dbq, dbk, dbv, gain_out,
+    q_s, k_s, v_s, g_s, kv_prev, pg_s, pg_r, own_s,
     gath, kf, vf, bias_w, bias_b, rs_s, rs_r, zsum, ry_s, ry_r,
     gl, gd_r, gz_s, gz_r, gy_s, gy_r,
-    in_sem, out_sem, kv_send, kv_recv, gath_send, gathy_recv, gathz_recv,
+    in_sem, kv_send, kv_recv, gath_send, gathy_recv, gathz_send, gathz_recv,
     pg_send, pg_recv, rs_send, rs_recv, ry_send, ry_recv,
     gd_send, gd_recv, gz_send, gz_recv, gy_send, gy_recv,
 ):
@@ -105,15 +107,17 @@
             bkv, gath.at[:, ctx], gath_send.at[0], gathy_recv.at[0], (dp, ypeer(j))
         ).start()
 
-    @pl.loop(0, heads)
+    def send_kv(h):
+        cols = pl.ds(pl.multiple_of(h * DH, DH), DH)
+        for i, source in enumerate((k_hbm, v_hbm)):
+            remote(
+                source.at[:, cols], kv_prev.at[h, i], kv_send.at[0], kv_recv.at[h],
+                (dp, after),
+            ).start()
+
+    @pl.loop(0, AHEAD)
     def _(h):
-        cols = pl.ds(pl.multiple_of(h * DH, DH), DH)
-        remote(
-            k_hbm.at[:, cols], kv_prev.at[h, 0], kv_send.at[0], kv_recv.at[h], (dp, after)
-        ).start()
-        remote(
-            v_hbm.at[:, cols], kv_prev.at[h, 1], kv_send.at[0], kv_recv.at[h], (dp, after)
-        ).start()
+        send_kv(h)
 
     width = window[0]
     for k in range(2):
@@ -137,14 +141,26 @@
 
     drain(gath.at[:, pl.ds(0, NY - 1)], gathy_recv.at[0])
     own_block.wait()
-    for g in range(groups):
-        @pl.loop(1, nz)
-        def _(j):
+
+    def spread(g):
+        @pl.loop(z + 1, nz)
+        def _(t):
             mine = pl.ds(z * NY, NY)
             remote(
-                gath.at[g, mine], gath.at[g, mine], gath_send.at[1], gathz_recv.at[g],
-                (dp, zpeer(j)),
+                gath.at[g, mine], gath.at[g, mine], gathz_send.at[t], gathz_recv.at[g, z],
+                (dp, t * NY + y),
             ).start()
+
+    spread(0)
+
+    @pl.loop(z + 1, nz)
+    def _(t):
+        gath[:, pl.ds(t * NY, NY)] = jnp.zeros((groups, NY, 16, DH), jnp.bfloat16)
+
+    @pl.loop(0, z)
+    def _(t):
+        rs_r[:, t] = jnp.zeros((heads, 16, DH), jnp.bfloat16)
+
 
     for load in loads:
         load.wait()
@@ -154,7 +170,14 @@
 
     @pl.loop(0, groups)
     def _(g):
-        drain(gath.at[0, pl.ds(0, (nz - 1) * NY)], gathz_recv.at[g])
+        @pl.loop(0, z)
+        def _(t):
+            drain(gath.at[g, pl.ds(t * NY, NY)], gathz_recv.at[g, t])
+
+        @pl.when(g + 1 < groups)
+        def _():
+            spread(g + 1)
+
         block = gath[g].astype(jnp.float32)
         kf[...] = block[:, 0:8].reshape(nctx * 8, DH)
         vf[...] = block[:, 8:16].reshape(nctx * 8, DH)
@@ -167,6 +190,11 @@
             gained = (raw_b * gain[pl.ds(h, 1), :]).astype(jnp.bfloat16)
             value_b = vf[pl.ds(hl, nb, stride=4), :].astype(jnp.bfloat16)
             drain(kv_prev.at[h], kv_recv.at[h])
+
+            @pl.when(h + AHEAD < heads)
+            def _():
+                send_kv(h + AHEAD)
+
             win_k = []
             win_v = []
             for k in range(2):
@@ -214,7 +242,7 @@
                 dk_b.append(dot_f(ds_b, q))
                 dv_b.append(dot_f(low_b, up))
                 dq = (dot_n(ds_w, win_k[k]) + dot_n(ds_b, gained)) * scale
-                dq_s[rows, cols] = dq[0:HALF].astype(jnp.bfloat16)
+                dq_out[rows, cols] = dq[0:HALF].astype(jnp.bfloat16)
                 gz_s[1 + k, pl.ds(h, 1), :] = dq[HALF : HALF + 1]
             for i, (t, c) in enumerate(((dk_w, scale), (dv_w, 1.0))):
                 pg_s[h, i, 0:HALF] = (t[0][0:HALF] * c).astype(jnp.bfloat16)
@@ -234,15 +262,12 @@
                 pg_s.at[h], pg_r.at[h], pg_send.at[0], pg_recv.at[h], (dp, before)
             ).start()
 
-            @pl.loop(1, nz)
-            def _(j):
+            @pl.loop(0, z)
+            def _(t):
                 remote(
-                    rs_s.at[h, (z + j) % nz], rs_r.at[h, z], rs_send.at[0], rs_recv.at[0],
-                    (dp, zpeer(j)),
+                    rs_s.at[h, t], rs_r.at[h, z], rs_send.at[t], rs_recv.at[z],
+                    (dp, t * NY + y),
                 ).start()
-
-    store_q = pltpu.make_async_copy(dq_s, dq_hbm, out_sem.at[0])
-    store_q.start()
 
     @pl.loop(1, ndp)
     def _(j):
@@ -253,7 +278,20 @@
     gd_r[dp] = gl[...]
     rs_r[:, z] = rs_s[:, z]
 
-    drain(rs_r.at[:, pl.ds(0, nz - 1)], rs_recv.at[0])
+    drain(gd_r.at[pl.ds(0, ndp - 1)], gd_recv.at[0])
+    gz_s[0] = jnp.sum(gd_r[...], axis=0)
+    gz_r[z] = gz_s[0]
+
+    @pl.loop(1, nz)
+    def _(j):
+        remote(
+            gz_s.at[0], gz_r.at[z], gz_send.at[0], gz_recv.at[0], (dp, zpeer(j))
+        ).start()
+
+    @pl.loop(z + 1, nz)
+    def _(t):
+        drain(rs_r.at[:, t], rs_recv.at[t])
+
     zsum[...] = jnp.sum(rs_r[...].astype(jnp.float32), axis=1).reshape(heads * 16, DH)
     for t in range(NY):
         for kv in range(2):
@@ -270,29 +308,16 @@
 
     ry_r[y] = ry_s[y]
 
-    drain(gd_r.at[pl.ds(0, ndp - 1)], gd_recv.at[0])
-    gz_s[0] = jnp.sum(gd_r[...], axis=0)
-    gz_r[z] = gz_s[0]
-
-    @pl.loop(1, nz)
-    def _(j):
-        remote(
-            gz_s.at[0], gz_r.at[z], gz_send.at[0], gz_recv.at[0], (dp, zpeer(j))
-        ).start()
-
-    @pl.loop(0, heads)
-    def _(h):
+    def finish(h):
         cols = pl.ds(pl.multiple_of(h * DH, DH), DH)
         drain(pg_r.at[h], pg_recv.at[h])
         total = own_s[h] + pg_r[h].astype(jnp.float32)
-        out_s[0, :, cols] = total[0].astype(jnp.bfloat16)
-        out_s[1, :, cols] = total[1].astype(jnp.bfloat16)
-        pltpu.make_async_copy(
-            out_s.at[0, :, cols], dk_hbm.at[:, cols], out_sem.at[1]
-        ).start()
-        pltpu.make_async_copy(
-            out_s.at[1, :, cols], dv_hbm.at[:, cols], out_sem.at[2]
-        ).start()
+        dk_out[:, cols] = total[0].astype(jnp.bfloat16)
+        dv_out[:, cols] = total[1].astype(jnp.bfloat16)
+
+    @pl.loop(0, heads - LAST)
+    def _(h):
+        finish(h)
 
     drain(gz_r.at[pl.ds(0, nz - 1)], gz_recv.at[0])
     gy_s[...] = jnp.sum(gz_r[...], axis=0)
@@ -302,27 +327,41 @@
     def _(j):
         remote(gy_s, gy_r.at[y], gy_send.at[0], gy_recv.at[0], (dp, ypeer(j))).start()
 
+    @pl.loop(heads - LAST, heads)
+    def _(h):
+        finish(h)
+
     drain(ry_r.at[pl.ds(0, NY - 1)], ry_recv.at[0])
     own = jnp.sum(ry_r[...].astype(jnp.float32), axis=0)
-    for k in range(2):
-        small[k] = gz_s[1 + k].astype(jnp.bfloat16)
-        small[2 + k] = (own[k] * gain[...]).astype(jnp.bfloat16)
-        small[4 + k] = own[2 + k].astype(jnp.bfloat16)
+    for h in range(heads):
+        cols = slice(h * DH, (h + 1) * DH)
+        scaled = gain[h : h + 1]
+        rows_q = [gz_s[1 + k, h : h + 1] for k in range(2)]
+        rows_k = [own[k, h : h + 1] * scaled for k in range(2)]
+        rows_v = [own[2 + k, h : h + 1] for k in range(2)]
+        dbq[:, cols] = jnp.concatenate(rows_q, axis=0).astype(jnp.bfloat16)
+        dbk[:, cols] = jnp.concatenate(rows_k, axis=0).astype(jnp.bfloat16)
+        dbv[:, cols] = jnp.concatenate(rows_v, axis=0).astype(jnp.bfloat16)
     drain(gy_r.at[pl.ds(0, NY - 1)], gy_recv.at[0])
     gain_out[...] = jnp.sum(gy_r[...], axis=0)
 
     drain(gath.at[:, pl.ds(0, NY - 1)], gath_send.at[0])
-    drain(gath.at[:, pl.ds(0, (nz - 1) * NY)], gath_send.at[1])
+
+    @pl.loop(z + 1, nz)
+    def _(t):
+        drain(gath.at[:, pl.ds(0, NY)], gathz_send.at[t])
+
     drain(kv_prev, kv_send.at[0])
     drain(pg_s, pg_send.at[0])
-    drain(rs_s.at[:, pl.ds(0, nz - 1)], rs_send.at[0])
+
+    @pl.loop(0, z)
+    def _(t):
+        drain(rs_s.at[:, t], rs_send.at[t])
+
     drain(ry_s.at[pl.ds(0, NY - 1)], ry_send.at[0])
     drain(gd_r.at[pl.ds(0, ndp - 1)], gd_send.at[0])
     drain(gz_r.at[pl.ds(0, nz - 1)], gz_send.at[0])
     drain(gy_r.at[pl.ds(0, NY - 1)], gy_send.at[0])
-    store_q.wait()
-    drain(dk_hbm, out_sem.at[1])
-    drain(dv_hbm, out_sem.at[2])
 
 
 def on_device(
@@ -348,18 +387,18 @@
     vmem = pl.BlockSpec(memory_space=pltpu.VMEM)
     anyspace = pl.BlockSpec(memory_space=pl.ANY)
     dma = pltpu.SemaphoreType.DMA
-    big = jax.ShapeDtypeStruct((slab, hd), bf16)
+    few = jax.ShapeDtypeStruct((2, hd), bf16)
+    big = pltpu.VMEM((slab, hd), bf16)
     outs = pl.pallas_call(
         partial(kernel, ndp, nctx, heads),
         out_shape=(
             big, big, big,
-            jax.ShapeDtypeStruct((6, heads, DH), bf16),
+            few, few, few,
             jax.ShapeDtypeStruct((heads, DH), f32),
         ),
         in_specs=[pl.BlockSpec(memory_space=pltpu.SMEM)] + [anyspace] * 4 + [vmem] * 3,
-        out_specs=(anyspace, anyspace, anyspace, vmem, vmem),
+        out_specs=(vmem,) * 7,
         scratch_shapes=[
-            pltpu.VMEM((slab, hd), bf16),
             pltpu.VMEM((slab, hd), bf16),
             pltpu.VMEM((slab, hd), bf16),
             pltpu.VMEM((slab, hd), bf16),
@@ -368,7 +407,6 @@
             pltpu.VMEM((heads, 2, slab, DH), bf16),
             pltpu.VMEM((heads, 2, slab, DH), bf16),
             pltpu.VMEM((heads, 2, slab, DH), f32),
-            pltpu.VMEM((2, slab, hd), bf16),
             pltpu.VMEM((groups, nctx, 16, DH), bf16),
             pltpu.VMEM((nctx * 8, DH), f32),
             pltpu.VMEM((nctx * 8, DH), f32),
@@ -385,9 +423,10 @@
             pltpu.VMEM((nz, heads, DH), f32),
             pltpu.VMEM((heads, DH), f32),
             pltpu.VMEM((NY, heads, DH), f32),
-            dma((5,)), dma((3,)), dma((1,)), dma((heads,)), dma((2,)), dma((1,)),
-            dma((groups,)), dma((1,)), dma((heads,)), dma((1,)), dma((1,)), dma((1,)),
-            dma((1,)), dma((1,)), dma((1,)), dma((1,)), dma((1,)), dma((1,)), dma((1,)),
+            dma((5,)), dma((1,)), dma((heads,)), dma((1,)), dma((1,)),
+            dma((nz,)), dma((groups, nz)), dma((1,)), dma((heads,)),
+            dma((nz,)), dma((nz,)), dma((1,)), dma((1,)),
+            dma((1,)), dma((1,)), dma((1,)), dma((1,)), dma((1,)), dma((1,)),
         ],
         compiler_params=pltpu.CompilerParams(
             collective_id=0, has_side_effects=True, vmem_limit_bytes=56 * 1024 * 1024
@@ -397,9 +436,7 @@
         window, queries[0], raw_keys[0], raw_values[0], upstream[0], bkv, bqg,
         key_gain.reshape(heads, DH),
     )
-    dq, dk, dv, small, gain = outs
-    small = small.reshape(3, 1, 2, hd)
-    return dq[None], dk[None], dv[None], small[0], small[1], small[2], gain.reshape(hd)
+    return tuple(out[None] for out in outs[:6]) + (outs[6].reshape(hd),)
 
 
 def solution(mesh):

time: 126 us -> 96.4 us (0.77)
  the two profiles are of different devices: /device:TPU:2 before, /device:TPU:42 now
where the time goes in v1:
time: 96.4 us; the launch traced here: 95.9 us
  Pallas kernels  86.8 us (90%)
  local copies, waits for them, and re-layouts  6.46 us (7%)
  between operations  1.35 us (1%)
  other arithmetic  1.23 us (1%)
    pallas_call x1, Pallas kernels, on_device(): pl.pallas_call(partial(kernel, ndp, nctx, heads), out_shape=(big, big, bi...  86.8 us
    unnamed x23, local copies, waits for them, and re-layouts  6.41 us

profile of v1, /device:TPU:42, one launch (start us, length us, event | category | flops | bytes accessed | tf_op | source)
XLA Modules:
  0.0 95.9 jit_solution(18017084001863176975)
XLA Ops:
  0.6 0.0 copy-start
  1.3 0.0 copy-done
  1.3 0.0 copy-start.1
  1.4 0.7 copy-done.1
  2.1 0.0 copy-start.6
  2.1 0.0 copy-start.7
  2.1 0.6 pad_maximum_fusion.bkv
  2.7 0.1 copy-done.6
  2.8 0.0 copy-done.7
  2.8 0.6 maximum_convert_fusion.bqg
  3.4 86.8 %beacon_backward.1 = (bf16[256,2048]{1,0:T(8,128)(2,1)S(1)}, bf16[256,2048]{1,0:T(8,128)(2,1)S(1)}, bf16[256,2048]{1,0:T(8,128)(2,1)S(1)}, bf16[2,2048]{1,0:T(2,...) custom-call(s32[1]{0:T(128)S(6)} %copy.33.window, bf16[256,2048]{1,0:T(8,128)(2,1)} %bitcast.29, ...), custom_call_target="tpu_custom_call" | custom-call | tf_op jit(solution)/shard_map/beacon_backward/pallas_call | solution.py:392
  90.3 1.0 %copy.30 = bf16[1,256,2048]{2,1,0:T(8,128)(2,1)} copy(bf16[1,256,2048]{2,1,0:T(8,128)(2,1)S(1)} %bitcast.28) | data formatting | bytes 2097152
  91.2 1.0 %copy.31 = bf16[1,256,2048]{2,1,0:T(8,128)(2,1)} copy(bf16[1,256,2048]{2,1,0:T(8,128)(2,1)S(1)} %bitcast.27) | data formatting | bytes 2097152
  92.2 0.0 copy-start.5
  92.2 1.0 %copy.32 = bf16[1,256,2048]{2,1,0:T(8,128)(2,1)} copy(bf16[1,256,2048]{2,1,0:T(8,128)(2,1)S(1)} %bitcast.26) | data formatting | bytes 2097152
  93.2 0.0 copy-done.5
  93.2 0.0 copy-start.4
  93.2 0.6 copy.34
  93.8 0.1 copy-done.4
  93.9 0.0 copy-start.3
  93.9 0.6 copy.35
  94.5 0.1 copy-done.3
  94.6 0.0 copy-start.2
  94.6 0.6 copy.36
  95.2 0.1 copy-done.2
  95.3 0.6 copy.37
  (5 shorter events, 0.0 us)
Async XLA Ops:
  0.6 0.7 copy-start
  1.3 0.7 copy-start.1
  2.1 0.7 copy-start.6
  2.1 0.7 copy-start.7
  92.2 1.0 %copy-start.5 = (bf16[2,2048]{1,0:T(2,128)(2,1)S(1)}, bf16[2,2048]{1,0:T(2,128)(2,1)}, u32[]{:S(2)}) copy-start(bf16[2,2048]{1,0:T(2,128)(2,1)} %get-tuple-element.17) | copy-start | bytes 24580
  93.2 0.7 copy-start.4
  93.9 0.7 copy-start.3
  94.6 0.7 copy-start.2

commit v2 on v1

--- a/solution.py
+++ b/solution.py
@@ -35,9 +35,9 @@
 
 def kernel(
     ndp, nctx, heads, window,
-    q_hbm, k_hbm, v_hbm, g_hbm, bkv, bqg, gain,
+    q_hbm, k_hbm, v_hbm, g_hbm, bq, bk, bv, bg, gain,
     dq_out, dk_out, dv_out, dbq, dbk, dbv, gain_out,
-    q_s, k_s, v_s, g_s, kv_prev, pg_s, pg_r, own_s,
+    q_s, k_s, v_s, g_s, kv_prev, pg_s, pg_r, own_s, bkv, bqg, stage,
     gath, kf, vf, bias_w, bias_b, rs_s, rs_r, zsum, ry_s, ry_r,
     gl, gd_r, gz_s, gz_r, gy_s, gy_r,
     in_sem, kv_send, kv_recv, gath_send, gathy_recv, gathz_send, gathz_recv,
@@ -78,6 +78,17 @@
     ]
     for load in loads:
         load.start()
+    for i, source in enumerate((bk, bv, bq, bg)):
+        wide = source[...].astype(jnp.float32)
+        for h in range(heads):
+            for k in range(2):
+                piece = wide[k : k + 1, h * DH : (h + 1) * DH]
+                if i < 2:
+                    at = i * 8 + k * 4 + h % 4
+                    stage[h // 4, at : at + 1] = piece
+                else:
+                    bqg[(i - 2) * 2 + k, h : h + 1] = piece
+    bkv[...] = stage[...].astype(jnp.bfloat16)
     own_block = pltpu.make_async_copy(bkv, gath.at[:, ctx], in_sem.at[4])
     own_block.start()
 
@@ -364,6 +375,17 @@
     drain(gy_r.at[pl.ds(0, NY - 1)], gy_send.at[0])
 
 
+def write_out(*refs):
+    sems = refs[14]
+    copies = [
+        pltpu.make_async_copy(refs[i], refs[7 + i], sems.at[i]) for i in range(7)
+    ]
+    for copy in copies:
+        copy.start()
+    for copy in copies:
+        copy.wait()
+
+
 def on_device(
     queries, raw_keys, raw_values, beacon_queries, beacon_keys, beacon_values,
     upstream, beacon_upstream, key_gain, window,
@@ -378,25 +400,17 @@
     groups = heads // 4
     bf16, f32 = jnp.bfloat16, jnp.float32
 
-    def grouped(block):
-        return block.reshape(2, groups, 4, DH).transpose(1, 0, 2, 3).reshape(groups, 8, DH)
-
-    bkv = jnp.concatenate([grouped(beacon_keys), grouped(beacon_values)], axis=1)
-    bqg = jnp.concatenate([beacon_queries[0], beacon_upstream[0]], axis=0)
-    bqg = bqg.astype(f32).reshape(4, heads, DH)
     vmem = pl.BlockSpec(memory_space=pltpu.VMEM)
     anyspace = pl.BlockSpec(memory_space=pl.ANY)
     dma = pltpu.SemaphoreType.DMA
-    few = jax.ShapeDtypeStruct((2, hd), bf16)
+    few = pltpu.VMEM((2, hd), bf16)
     big = pltpu.VMEM((slab, hd), bf16)
     outs = pl.pallas_call(
         partial(kernel, ndp, nctx, heads),
         out_shape=(
-            big, big, big,
-            few, few, few,
-            jax.ShapeDtypeStruct((heads, DH), f32),
+            big, big, big, few, few, few, pltpu.VMEM((heads, DH), f32),
         ),
-        in_specs=[pl.BlockSpec(memory_space=pltpu.SMEM)] + [anyspace] * 4 + [vmem] * 3,
+        in_specs=[pl.BlockSpec(memory_space=pltpu.SMEM)] + [anyspace] * 4 + [vmem] * 5,
         out_specs=(vmem,) * 7,
         scratch_shapes=[
             pltpu.VMEM((slab, hd), bf16),
@@ -407,6 +421,9 @@
             pltpu.VMEM((heads, 2, slab, DH), bf16),
             pltpu.VMEM((heads, 2, slab, DH), bf16),
             pltpu.VMEM((heads, 2, slab, DH), f32),
+            pltpu.VMEM((groups, 16, DH), bf16),
+            pltpu.VMEM((4, heads, DH), f32),
+            pltpu.VMEM((groups, 16, DH), f32),
             pltpu.VMEM((groups, nctx, 16, DH), bf16),
             pltpu.VMEM((nctx * 8, DH), f32),
             pltpu.VMEM((nctx * 8, DH), f32),
@@ -433,9 +450,19 @@
         ),
         name="beacon_backward",
     )(
-        window, queries[0], raw_keys[0], raw_values[0], upstream[0], bkv, bqg,
+        window, queries[0], raw_keys[0], raw_values[0], upstream[0],
+        beacon_queries[0], beacon_keys[0], beacon_values[0], beacon_upstream[0],
         key_gain.reshape(heads, DH),
     )
+    plain = [jax.ShapeDtypeStruct(out.shape, out.dtype) for out in outs]
+    outs = pl.pallas_call(
+        write_out,
+        out_shape=plain,
+        in_specs=[anyspace] * 7,
+        out_specs=[anyspace] * 7,
+        scratch_shapes=[dma((7,))],
+        name="write_out",
+    )(*[pltpu.with_memory_space_constraint(out, pltpu.VMEM) for out in outs])
     return tuple(out[None] for out in outs[:6]) + (outs[6].reshape(hd),)
 
 

time: 96.4 us -> 89.8 us (0.932)
  local copies, waits for them, and re-layouts: 6.46 us -> 0 us
  Pallas kernels: 86.8 us -> 88.3 us
  other arithmetic: 1.23 us -> 0 us
    unnamed x23 -> x0, local copies, waits for them, and re-layouts: 6.41 us -> none
    pallas_call x0 -> x1, Pallas kernels: none -> 1.73 us  [on_device(): pl.pallas_call(write_out, out_shape=plain, in_specs=[anyspace] * 7, out_s...]
where the time goes in v2:
time: 89.8 us; the launch traced here: 89.6 us
  Pallas kernels  88.3 us (98%)
  between operations  1.29 us (1%)
    pallas_call x1, Pallas kernels, on_device(): pl.pallas_call(partial(kernel, ndp, nctx, heads), out_shape=(big, big, bi...  86.5 us

profile of v2, /device:TPU:42, one launch (start us, length us, event | category | flops | bytes accessed | tf_op | source)
XLA Modules:
  0.0 89.6 jit_solution(17717146074021615607)
XLA Ops:
  1.3 86.5 %beacon_backward.1 = (bf16[256,2048]{1,0:T(8,128)(2,1)S(1)}, bf16[256,2048]{1,0:T(8,128)(2,1)S(1)}, bf16[256,2048]{1,0:T(8,128)(2,1)S(1)}, bf16[2,2048]{1,0:T(2,...) custom-call(s32[1]{0:T(128)S(6)} %copy.17.window, ...), custom_call_target="tpu_custom_call" | custom-call | tf_op jit(solution)/shard_map/beacon_backward/pallas_call | solution.py:408
  87.8 1.7 %write_out.1 = (bf16[256,2048]{1,0:T(8,128)(2,1)}, bf16[256,2048]{1,0:T(8,128)(2,1)}, bf16[256,2048]{1,0:T(8,128)(2,1)}, bf16[2,2048]{1,0:T(2,128)(2,1)}, bf16[2...) custom-call(bf16[256,2048]{1,0:T(8,128)(2,1)S(1)} %get-tuple-element.21.refs_0_, ...), custom_call_target="tpu_custom_call" | custom-call | tf_op jit(solution)/shard_map/write_out/pallas_call | solution.py:458

commit v3 on v2

--- a/solution.py
+++ b/solution.py
@@ -12,7 +12,7 @@
 NY = 4
 HALF = 128
 ROWS = 144
-AHEAD = 2
+AHEAD = 4
 LAST = 3
 WCOLS = 384
 MESH = pl.DeviceIdType.MESH

time: 89.8 us -> 92 us (1.024)
  Pallas kernels: 88.3 us -> 90.5 us
    pallas_call x1, Pallas kernels: 86.5 us -> 88.8 us  [on_device(): pl.pallas_call(partial(kernel, ndp, nctx, heads), out_shape=(big, big, bi...]
where the time goes in v3:
time: 92 us; the launch traced here: 91.8 us
  Pallas kernels  90.5 us (98%)
  between operations  1.29 us (1%)
    pallas_call x1, Pallas kernels, on_device(): pl.pallas_call(partial(kernel, ndp, nctx, heads), out_shape=(big, big, bi...  88.8 us

profile of v3, /device:TPU:42, one launch (start us, length us, event | category | flops | bytes accessed | tf_op | source)
XLA Modules:
  0.0 91.8 jit_solution(7398109704766083532)
XLA Ops:
  1.3 88.8 %beacon_backward.1 = (bf16[256,2048]{1,0:T(8,128)(2,1)S(1)}, bf16[256,2048]{1,0:T(8,128)(2,1)S(1)}, bf16[256,2048]{1,0:T(8,128)(2,1)S(1)}, bf16[2,2048]{1,0:T(2,...) custom-call(s32[1]{0:T(128)S(6)} %copy.17.window, ...), custom_call_target="tpu_custom_call" | custom-call | tf_op jit(solution)/shard_map/beacon_backward/pallas_call | solution.py:408
  90.0 1.7 %write_out.1 = (bf16[256,2048]{1,0:T(8,128)(2,1)}, bf16[256,2048]{1,0:T(8,128)(2,1)}, bf16[256,2048]{1,0:T(8,128)(2,1)}, bf16[2,2048]{1,0:T(2,128)(2,1)}, bf16[2...) custom-call(bf16[256,2048]{1,0:T(8,128)(2,1)S(1)} %get-tuple-element.21.refs_0_, ...), custom_call_target="tpu_custom_call" | custom-call | tf_op jit(solution)/shard_map/write_out/pallas_call | solution.py:458
